TPU v7x, 512 devices: a whole 4x4x16 slice. The times are simulated.
512 devices in a mesh: blk: 64 (over x, z), head: 8 (over y, core).
Axes of the slice: x: 4, y: 4, z: 16, core: 2. Of those that a mesh axis runs over, the one named last changes fastest.
Arguments:
- acceptance_vector: bfloat16 [8192, 4096], P('blk', 'head'), may hold values from -6 to 6
- lookup_vector_array: bfloat16 [8192, 4096], P('blk', 'head'), may hold values from -2 to 2
- payload_vector_array: bfloat16 [8192, 4096], P('blk', 'head'), may hold values from -6 to 6
- raw_gating_signal: bfloat16 [8192, 4096], P('blk', 'head'), may hold values from -6 to 6
- raw_forgetting_rate: bfloat16 [8192, 4096], P('blk', 'head'), may hold values from -16 to 1
- current_reward_vector: float32 [4096], P('head'), may hold values from -1.5 to 1.5
- memory_following_query: bfloat16 [2, 4096, 64], P(None, 'head'), may hold values from -24 to 24
- group_layernorm_scaling: float32 [4096], P('head'), may hold values from 0.25 to 1.75
- closing_layernorm_scaling: float32 [4096], replicated, may hold values from 0.25 to 1.75
- skip_stream_input: bfloat16 [8192, 4096], P(('blk', 'head')), may hold values from -6 to 6
- closing_projection: bfloat16 [4096, 4096], P('head', 'blk'), may hold values from -0.09375 to 0.09375
- vocabulary_readout: bfloat16 [32768, 4096], P('blk'), may hold values from -15.625 to 15.625
- following_labels: int32 [8192], P(('blk', 'head')), may hold values from 0 to 32767
- response_indicator: int32 [8192], P(('blk', 'head')), may hold values 0 or 1
- baseline_logarithmic_likelihood: float32 [8192], P(('blk', 'head')), may hold values from -14 to -6
- rollout_for_segment: int32 [64], replicated, may hold values from 0 to 15, never falling along the last dimension, each value on 1 to 32 neighbouring positions
- query_text_for_rollout: int32 [16], replicated, may hold values from 0 to 1
Outputs:
- token_ratio: float32 [8192], P(('blk', 'head'))
- seq_ratio: float32 [16], replicated
Inputs may be any that keep to these rules, and one draw needn't show every extreme that they name: `rollout_for_segment`: sequences fill whole consecutive blocks, each 1 to 32 blocks, one exactly 32; ids start at 0 and rise by one at each new sequence.
All inputs are finite; a program needn't handle non-finite values. No bound on the sum of `response_indicator` on one device may be relied on, other than what follows from the above.
Results may differ from a plain program's by a relative error of at most 0.0017.
Values may be sent and summed in bfloat16 or wider, within the bound.
No kernel may reach another device: no remote copies, remote signals or barrier semaphores. Data moves between devices by JAX's collectives and lax.ppermute only.
A program may use at most 128 MiB of HBM per device.

v0:
```python
import jax
import jax.numpy as jnp
from jax import lax
from jax.sharding import PartitionSpec as P

GROUP_DIMENSION = 64
TOK_BLK = 128


def passed_along(value, axis, steps):
    count = lax.axis_size(axis)
    first, last = (max(0, -steps), min(count, count - steps))
    return lax.ppermute(value, axis, [(source, source + steps) for source in range(first, last)])


def joined(part, axis, combine):
    gathered = jax.tree.map(lambda a: lax.all_gather(a, axis), part)

    def take(source):
        return jax.tree.map(lambda a: lax.dynamic_index_in_dim(a, source, 0, False), gathered)

    return lax.fori_loop(
        1, lax.axis_size(axis), lambda source, state: combine(state, take(source)), take(0)
    )


def per_device(
    acceptance_vector,
    lookup_vector_array,
    payload_vector_array,
    raw_gating_signal,
    raw_forgetting_rate,
    current_reward_vector,
    memory_following_query,
    group_layernorm_scaling,
    closing_layernorm_scaling,
    skip_stream_input,
    closing_projection,
    vocabulary_readout,
    following_labels,
    response_indicator,
    baseline_logarithmic_likelihood,
    rollout_for_segment,
    query_text_for_rollout,
):
    n_blk = lax.axis_size("blk")
    blk_index = lax.axis_index("blk")
    rows, width = acceptance_vector.shape
    local_attention_groups = width // GROUP_DIMENSION
    sub = 16
    nsub = rows // sub
    highest = lax.Precision.HIGHEST

    def split(a):
        return (
            a.astype(jnp.float32)
            .reshape(nsub, sub, local_attention_groups, GROUP_DIMENSION)
            .transpose(0, 2, 1, 3)
        )

    inherited_memory = split(acceptance_vector)
    lookup_vectors = split(lookup_vector_array)
    vals = split(payload_vector_array)
    log_decay = -jnp.exp(split(raw_forgetting_rate))
    inclusive = jnp.cumsum(log_decay, axis=2)
    exclusive = inclusive - log_decay
    last = inclusive[:, :, -1, :]
    this_seq = rollout_for_segment[blk_index]
    prev_seq = rollout_for_segment[jnp.maximum(blk_index - 1, 0)]
    starts = jnp.logical_or(blk_index == 0, this_seq != prev_seq).astype(jnp.float32)
    prompt = (
        memory_following_query[query_text_for_rollout[this_seq]]
        .astype(jnp.float32)
        .reshape(local_attention_groups, GROUP_DIMENSION, GROUP_DIMENSION)
    )
    later = jnp.arange(sub)[:, None] > jnp.arange(sub)[None, :]
    spread = exclusive[:, :, :, None, :] - inclusive[:, :, None, :, :]
    weights = jnp.where(later[None, None, :, :, None], jnp.exp(jnp.minimum(spread, 0.0)), 0.0)
    scores = jnp.sum(
        inherited_memory[:, :, :, None, :] * lookup_vectors[:, :, None, :, :] * weights, axis=-1
    )
    group_current_reward = current_reward_vector.reshape(local_attention_groups, GROUP_DIMENSION)
    diagonal_term = jnp.sum(
        inherited_memory * lookup_vectors * group_current_reward[None, :, None, :], axis=-1
    )
    wkv = (
        jnp.einsum("nhts,nhsj->nhtj", scores, vals, precision=highest)
        + diagonal_term[..., None] * vals
    )
    keys_late = lookup_vectors * jnp.exp(last[:, :, None, :] - inclusive)
    delta = jnp.einsum("nhsi,nhsj->nhij", keys_late, vals, precision=highest)

    def advance(state, item):
        change, fall = item
        return (jnp.exp(fall)[:, :, None] * state + change, state)

    end_state, entering = lax.scan(advance, starts * prompt, (delta, last))
    wkv = wkv + jnp.einsum(
        "nhti,nhij->nhtj", inherited_memory * jnp.exp(exclusive), entering, precision=highest
    )
    block_fall = jnp.exp(jnp.sum(last, axis=0)) * (1.0 - starts)

    def relay_step(step, incoming):
        leaving = block_fall[:, :, None] * incoming + end_state
        return passed_along(leaving, "blk", 1)

    incoming = lax.fori_loop(0, n_blk // 2 - 1, relay_step, jnp.zeros_like(end_state))
    offsets = jnp.cumsum(last, axis=0) - last
    carried = inherited_memory * jnp.exp(exclusive + offsets[:, :, None, :])
    wkv = wkv + (1.0 - starts) * jnp.einsum("nhti,hij->nhtj", carried, incoming, precision=highest)
    mean = jnp.mean(wkv, axis=-1, keepdims=True)
    var = jnp.mean((wkv - mean) ** 2, axis=-1, keepdims=True)
    normal_h = (wkv - mean) / jnp.sqrt(var + 0.00064)
    normal_h = normal_h.transpose(0, 2, 1, 3).reshape(rows, width) * group_layernorm_scaling
    mixed = (normal_h * jax.nn.silu(raw_gating_signal.astype(jnp.float32))).astype(jnp.bfloat16)
    partial_out = jnp.dot(
        mixed,
        lax.all_gather(closing_projection, "blk", axis=1, tiled=True),
        preferred_element_type=jnp.float32,
    )
    own_rows = lax.psum_scatter(partial_out, "head", scatter_dimension=0, tiled=True)
    hidden = skip_stream_input.astype(jnp.float32) + own_rows
    hmean = jnp.mean(hidden, axis=-1, keepdims=True)
    hvar = jnp.mean((hidden - hmean) ** 2, axis=-1, keepdims=True)
    normed = ((hidden - hmean) / jnp.sqrt(hvar + 1e-05) * closing_layernorm_scaling).astype(
        jnp.bfloat16
    )
    local_rows = normed.shape[0]
    vocab_local = vocabulary_readout.shape[0]
    vocab_base = blk_index * vocab_local
    rows_n = lax.all_gather(normed, "blk", axis=0, tiled=True)
    rows_t = lax.all_gather(following_labels, "blk", axis=0, tiled=True)
    logits = lax.dot_general(
        rows_n, vocabulary_readout, (((1,), (1,)), ((), ())), preferred_element_type=jnp.float32
    )
    top = jnp.max(logits, axis=1)
    grand_sum = jnp.sum(jnp.exp(logits - top[:, None]), axis=1)
    entry = jnp.arange(vocab_local, dtype=jnp.int32)[None, :] + vocab_base
    picked = jnp.sum(jnp.where(entry == rows_t[:, None], logits, 0.0), axis=1)
    top, grand_sum, picked = tuple((new for new in (top, grand_sum, picked)))

    def join(first, second):
        peak = jnp.maximum(first[0], second[0])
        summed = first[1] * jnp.exp(first[0] - peak) + second[1] * jnp.exp(second[0] - peak)
        return (peak, summed, first[2] + second[2])

    top, grand_sum, picked = joined((top, grand_sum, picked), "blk", join)
    logp = picked - top - jnp.log(grand_sum)
    mine = lax.dynamic_slice_in_dim(logp, blk_index * local_rows, local_rows)
    token_ratio = response_indicator.astype(jnp.float32) * (mine - baseline_logarithmic_likelihood)
    seq_count = query_text_for_rollout.shape[0]
    marker = (jnp.arange(seq_count, dtype=jnp.int32) == this_seq).astype(jnp.float32)
    partial_seq = marker * (jnp.sum(token_ratio) / TOK_BLK)
    seq_ratio = lax.psum(partial_seq, ("blk", "head"))
    return (token_ratio, seq_ratio)


def solution(mesh):
    placed = (
        P("blk", "head"),
        P("blk", "head"),
        P("blk", "head"),
        P("blk", "head"),
        P("blk", "head"),
        P("head"),
        P(None, "head", None),
        P("head"),
        P(),
        P(("blk", "head"), None),
        P("head", "blk"),
        P("blk", None),
        P(("blk", "head")),
        P(("blk", "head")),
        P(("blk", "head")),
        P(),
        P(),
    )
    return jax.shard_map(
        per_device, mesh=mesh, in_specs=placed, out_specs=(P(("blk", "head")), P()), check_vma=False
    )
```

profile of v0, /device:TPU:1, one launch (start us, length us, event | category | flops | bytes accessed | tf_op | source)
XLA Modules:
  0.0 976.3 jit_solution(5648357997811550387)
XLA Ops:
  25.3 7.4 while.41
  41.9 301.2 %while.42 = (s32[]{:T(128)}, f32[8,64,64]{2,1,0:T(8,128)S(1)}, f32[8,64]{1,0:T(8,128)S(1)}, f32[8,64,64]{2,1,0:T(8,128)S(1)}, s32[]{:T(128)}) while((s32[]{:T(128)}, f32[8,64,64]{2,1,0:T(8,128)S(1)}, f32[8,64]{1,0:T(8,128)S(1)}, f32[8,64,64]{2,1,0:T(8,128)S(1)}, s32[]{:T(128)}) %tuple.86), condition=%wide.region_7.8_spmd, body=%wide.region_6.7_spmd.sunk | while | flops 65538 | bytes 919653 | solution.py:107
  50.2 5.4 collective-permute-start
  76.6 5.9 collective-permute-start
  104.6 5.6 collective-permute-start
  114.3 8.7 collective-permute-start
  123.0 8.9 collective-permute-done
  136.3 7.5 collective-permute-done
  143.9 5.6 collective-permute-start
  149.6 7.7 collective-permute-done
  181.8 5.5 collective-permute-start
  190.7 5.3 collective-permute-start
  199.4 5.5 collective-permute-start
  217.2 5.3 collective-permute-start
  227.5 5.5 collective-permute-start
  233.0 5.7 collective-permute-done
  238.9 6.0 collective-permute-start
  275.3 5.3 collective-permute-start
  284.0 5.3 collective-permute-start
  301.5 5.3 collective-permute-start
  311.6 5.6 collective-permute-start
  317.2 5.7 collective-permute-done
  323.1 6.0 collective-permute-start
  350.4 98.3 %reduce-scatter.2.cloned.1.call-done = f32[16,4096]{1,0:T(8,128)} async-done(((f32[128,4096]{1,0:T(8,128)}), f32[16,4096]{1,0:T(8,128)}) %reduce-scatter.2.cloned.1.call-update) | async-done | bytes 262160 | tf_op jit(solution)/shard_map/reduce_scatter | solution.py:121
  454.9 23.9 %all-reduce = s32[1024]{0:T(1024)S(1)} all-reduce(s32[1024]{0:T(1024)S(1)} %dynamic-update-slice), channel_id=1, replica_groups=mesh['blk'=64,'head'=8] {'blk'}, use_global_device_ids=true, to_apply=%add | all-reduce | flops 1024 | bytes 8192
  478.8 124.2 %all-gather.8.cloned.1.call-done = bf16[1024,4096]{1,0:T(8,128)(2,1)} async-done(((bf16[16,4096]{1,0:T(8,128)(2,1)}), bf16[1024,4096]{1,0:T(8,128)(2,1)}) %all-gather.8.cloned.1.call-update) | async-done | bytes 8388624 | tf_op jit(solution)/shard_map/all_gather | solution.py:131
  603.0 8.2 fusion.38
  611.8 61.3 %all-gather.1 = f32[65536]{0:T(1024)S(1)} all-gather(f32[1024]{0:T(1024)S(1)} %get-tuple-element.237), channel_id=3, replica_groups=mesh['blk'=64,'head'=8] {'blk'}, dimensions={0}, use_global_device_ids=true | all-gather | bytes 266240 | tf_op jit(solution)/shard_map/all_gather | solution.py:17
  673.2 63.6 %all-gather.2 = f32[65536]{0:T(1024)S(1)} all-gather(f32[1024]{0:T(1024)S(1)} %get-tuple-element.236), channel_id=4, replica_groups=mesh['blk'=64,'head'=8] {'blk'}, dimensions={0}, use_global_device_ids=true | all-gather | bytes 266240 | tf_op jit(solution)/shard_map/all_gather | solution.py:17
  736.8 63.0 %all-gather = f32[65536]{0:T(1024)S(1)} all-gather(f32[1024]{0:T(1024)S(1)} %get-tuple-element.289), channel_id=2, replica_groups=mesh['blk'=64,'head'=8] {'blk'}, dimensions={0}, use_global_device_ids=true | all-gather | bytes 266240 | tf_op jit(solution)/shard_map/all_gather | solution.py:17
  799.9 5.9 while.43
  808.4 161.3 %psum.7 = f32[16]{0:T(128)} all-reduce(f32[16]{0:T(128)S(1)} %compare_select_fusion), channel_id=1, replica_groups=mesh['blk'=64,'head'=8] {'blk','head'}, use_global_device_ids=true, to_apply=%region_20.21 | all-reduce | flops 16 | bytes 128 | tf_op jit(solution)/shard_map/psum | solution.py:154
  (449 shorter events, 220.1 us)
Async XLA Ops:
  7.2 338.0 %all-gather.6.cloned.1.call-start = ((), (), s32[]{:S(2)}) async-start(), calls=%async_computation.1 | async-start | bytes 4259840 | tf_op jit(solution)/shard_map/all_gather | solution.py:118
  7.9 440.7 %reduce-scatter.2.cloned.1.call-start = ((), (), s32[]{:S(2)}) async-start(), calls=%async_computation.2 | async-start | bytes 2359296 | tf_op jit(solution)/shard_map/reduce_scatter | solution.py:121
  42.0 8.0 collective-permute-start
  50.2 9.0 collective-permute-start
  59.4 8.7 collective-permute-start
  68.2 8.3 collective-permute-start
  76.6 9.4 collective-permute-start
  86.2 8.5 collective-permute-start
  94.8 9.6 collective-permute-start
  104.6 9.6 collective-permute-start
  114.3 17.5 %collective-permute-start = (f32[8,64,64]{2,1,0:T(8,128)S(1)}, f32[8,64,64]{2,1,0:T(8,128)S(1)}, u32[]{:S(2)}, u32[]{:S(2)}) collective-permute-start(f32[8,64,64]{2,1,0:T(8,128)S(1)} %multiply_add_fusion.4), channel_id=1, source_target_pairs={{0,8},{8,16},{16,24},{24,32},{32,40},{40,48},{48,56},{56,64},{64,7... | collective-permute-start | bytes 393224 | tf_op jit(solution)/shard_map/while/body/eval_jaxpr/ppermute | solution.py:13
  132.0 11.8 %collective-permute-start = (f32[8,64,64]{2,1,0:T(8,128)S(1)}, f32[8,64,64]{2,1,0:T(8,128)S(1)}, u32[]{:S(2)}, u32[]{:S(2)}) collective-permute-start(f32[8,64,64]{2,1,0:T(8,128)S(1)} %multiply_add_fusion.4), channel_id=1, source_target_pairs={{0,8},{8,16},{16,24},{24,32},{32,40},{40,48},{48,56},{56,64},{64,7... | collective-permute-start | bytes 393224 | tf_op jit(solution)/shard_map/while/body/eval_jaxpr/ppermute | solution.py:13
  143.9 13.4 %collective-permute-start = (f32[8,64,64]{2,1,0:T(8,128)S(1)}, f32[8,64,64]{2,1,0:T(8,128)S(1)}, u32[]{:S(2)}, u32[]{:S(2)}) collective-permute-start(f32[8,64,64]{2,1,0:T(8,128)S(1)} %multiply_add_fusion.4), channel_id=1, source_target_pairs={{0,8},{8,16},{16,24},{24,32},{32,40},{40,48},{48,56},{56,64},{64,7... | collective-permute-start | bytes 393224 | tf_op jit(solution)/shard_map/while/body/eval_jaxpr/ppermute | solution.py:13
  157.4 8.5 collective-permute-start
  173.7 7.9 collective-permute-start
  181.8 8.8 collective-permute-start
  190.7 8.6 collective-permute-start
  199.4 8.8 collective-permute-start
  208.4 8.7 collective-permute-start
  217.2 10.1 %collective-permute-start = (f32[8,64,64]{2,1,0:T(8,128)S(1)}, f32[8,64,64]{2,1,0:T(8,128)S(1)}, u32[]{:S(2)}, u32[]{:S(2)}) collective-permute-start(f32[8,64,64]{2,1,0:T(8,128)S(1)} %multiply_add_fusion.4), channel_id=1, source_target_pairs={{0,8},{8,16},{16,24},{24,32},{32,40},{40,48},{48,56},{56,64},{64,7... | collective-permute-start | bytes 393224 | tf_op jit(solution)/shard_map/while/body/eval_jaxpr/ppermute | solution.py:13
  227.5 11.3 %collective-permute-start = (f32[8,64,64]{2,1,0:T(8,128)S(1)}, f32[8,64,64]{2,1,0:T(8,128)S(1)}, u32[]{:S(2)}, u32[]{:S(2)}) collective-permute-start(f32[8,64,64]{2,1,0:T(8,128)S(1)} %multiply_add_fusion.4), channel_id=1, source_target_pairs={{0,8},{8,16},{16,24},{24,32},{32,40},{40,48},{48,56},{56,64},{64,7... | collective-permute-start | bytes 393224 | tf_op jit(solution)/shard_map/while/body/eval_jaxpr/ppermute | solution.py:13
  238.9 11.2 %collective-permute-start = (f32[8,64,64]{2,1,0:T(8,128)S(1)}, f32[8,64,64]{2,1,0:T(8,128)S(1)}, u32[]{:S(2)}, u32[]{:S(2)}) collective-permute-start(f32[8,64,64]{2,1,0:T(8,128)S(1)} %multiply_add_fusion.4), channel_id=1, source_target_pairs={{0,8},{8,16},{16,24},{24,32},{32,40},{40,48},{48,56},{56,64},{64,7... | collective-permute-start | bytes 393224 | tf_op jit(solution)/shard_map/while/body/eval_jaxpr/ppermute | solution.py:13
  250.2 8.8 collective-permute-start
  266.7 8.4 collective-permute-start
  275.3 8.6 collective-permute-start
  284.0 8.6 collective-permute-start
  292.8 8.6 collective-permute-start
  301.5 9.9 %collective-permute-start = (f32[8,64,64]{2,1,0:T(8,128)S(1)}, f32[8,64,64]{2,1,0:T(8,128)S(1)}, u32[]{:S(2)}, u32[]{:S(2)}) collective-permute-start(f32[8,64,64]{2,1,0:T(8,128)S(1)} %multiply_add_fusion.4), channel_id=1, source_target_pairs={{0,8},{8,16},{16,24},{24,32},{32,40},{40,48},{48,56},{56,64},{64,7... | collective-permute-start | bytes 393224 | tf_op jit(solution)/shard_map/while/body/eval_jaxpr/ppermute | solution.py:13
  311.6 11.4 %collective-permute-start = (f32[8,64,64]{2,1,0:T(8,128)S(1)}, f32[8,64,64]{2,1,0:T(8,128)S(1)}, u32[]{:S(2)}, u32[]{:S(2)}) collective-permute-start(f32[8,64,64]{2,1,0:T(8,128)S(1)} %multiply_add_fusion.4), channel_id=1, source_target_pairs={{0,8},{8,16},{16,24},{24,32},{32,40},{40,48},{48,56},{56,64},{64,7... | collective-permute-start | bytes 393224 | tf_op jit(solution)/shard_map/while/body/eval_jaxpr/ppermute | solution.py:13
  323.1 11.3 %collective-permute-start = (f32[8,64,64]{2,1,0:T(8,128)S(1)}, f32[8,64,64]{2,1,0:T(8,128)S(1)}, u32[]{:S(2)}, u32[]{:S(2)}) collective-permute-start(f32[8,64,64]{2,1,0:T(8,128)S(1)} %multiply_add_fusion.4), channel_id=1, source_target_pairs={{0,8},{8,16},{16,24},{24,32},{32,40},{40,48},{48,56},{56,64},{64,7... | collective-permute-start | bytes 393224 | tf_op jit(solution)/shard_map/while/body/eval_jaxpr/ppermute | solution.py:13
  334.6 8.6 collective-permute-start
  350.3 252.6 %all-gather.8.cloned.1.call-start = ((), (), s32[]{:S(2)}) async-start(), calls=%async_computation.3 | async-start | bytes 8519680 | tf_op jit(solution)/shard_map/all_gather | solution.py:131
  (21 other events, 804.1 us)
Sparse Core Ops, SparseCore 0:
  11.0 147.0 all-gather.5
  350.5 98.1 reduce-scatter.1
  452.8 150.1 all-gather.7
where the time goes:
time: 978 us; the launch traced here: 976 us
  blocking collectives  373 us (38%)
  waiting for transfers between devices  357 us (37%)
  starting transfers between devices  163 us (17%)
  other arithmetic  24 us (2%)
  between operations  20.8 us (2%)
  matrix products  19.8 us (2%)
  local copies, waits for them, and re-layouts  14.7 us (2%)
    all_gather x3, blocking collectives, joined(): gathered = jax.tree.map(lambda a: lax.all_gather(a, axis), part)  188 us
    ppermute x31, starting transfers between devices, passed_along(): lax.ppermute(value, axis, [(source, source + steps) for source in range(f...  163 us
    psum x1, blocking collectives, per_device(): seq_ratio = lax.psum(partial_seq, ('blk', 'head'))  161 us
    ppermute x31, waiting for transfers between devices, passed_along(): lax.ppermute(value, axis, [(source, source + steps) for source in range(f...  134 us
    all_gather x1, waiting for transfers between devices, per_device(): rows_n = lax.all_gather(normed, 'blk', axis=0, tiled=True)  124 us
    reduce_scatter x1, waiting for transfers between devices, per_device(): lax.psum_scatter(partial_out, 'head', scatter_dimension=0, tiled=True)  98.3 us
    unnamed x1, blocking collectives  23.9 us
  transfers between devices with their start and end apart: 34, of which 33 were waited for; matrix products, arithmetic and copies ran while one was open for 4% of the time, Pallas kernels for 0%

commit v1 on v0

--- a/solution.py
+++ b/solution.py
@@ -151,7 +151,7 @@
     seq_count = query_text_for_rollout.shape[0]
     marker = (jnp.arange(seq_count, dtype=jnp.int32) == this_seq).astype(jnp.float32)
     partial_seq = marker * (jnp.sum(token_ratio) / TOK_BLK)
-    seq_ratio = lax.psum(partial_seq, ("blk", "head"))
+    seq_ratio = lax.psum(lax.psum(partial_seq, "blk"), "head")
     return (token_ratio, seq_ratio)
 
 

time: 978 us -> 1030 us (1.053)
  blocking collectives: 373 us -> 427 us
    psum x1 -> x2, blocking collectives: 161 us -> 215 us  [per_device(): seq_ratio = lax.psum(lax.psum(partial_seq, 'blk'), 'head')]
  transfers between devices with their start and end apart: 34 -> 34, of which waited for: 33 -> 33; matrix products, arithmetic and copies ran while one was open for 4% -> 3% of each run, Pallas kernels for 0% -> 0%
where the time goes in v1:
time: 1030 us
  blocking collectives  427 us (41%)
  waiting for transfers between devices  357 us (35%)
  starting transfers between devices  163 us (16%)
  other arithmetic  24 us (2%)
  between operations  20.8 us (2%)
  matrix products  19.8 us (2%)
  local copies, waits for them, and re-layouts  14.7 us (1%)
    psum x2, blocking collectives, per_device(): seq_ratio = lax.psum(lax.psum(partial_seq, 'blk'), 'head')  215 us
    all_gather x3, blocking collectives, joined(): gathered = jax.tree.map(lambda a: lax.all_gather(a, axis), part)  188 us
    ppermute x31, starting transfers between devices, passed_along(): lax.ppermute(value, axis, [(source, source + steps) for source in range(f...  163 us
    ppermute x31, waiting for transfers between devices, passed_along(): lax.ppermute(value, axis, [(source, source + steps) for source in range(f...  134 us
    all_gather x1, waiting for transfers between devices, per_device(): rows_n = lax.all_gather(normed, 'blk', axis=0, tiled=True)  124 us
    reduce_scatter x1, waiting for transfers between devices, per_device(): lax.psum_scatter(partial_out, 'head', scatter_dimension=0, tiled=True)  98.3 us
    unnamed x1, blocking collectives  23.9 us
  transfers between devices with their start and end apart: 34, of which 33 were waited for; matrix products, arithmetic and copies ran while one was open for 3% of the time, Pallas kernels for 0%

profile of v1, /device:TPU:1, one launch (start us, length us, event | category | flops | bytes accessed | tf_op | source)
XLA Modules:
  0.0 1030.0 jit_solution(1791483548409085827)
XLA Ops:
  25.3 7.4 while.41
  41.9 301.2 %while.42 = (s32[]{:T(128)}, f32[8,64,64]{2,1,0:T(8,128)S(1)}, f32[8,64]{1,0:T(8,128)S(1)}, f32[8,64,64]{2,1,0:T(8,128)S(1)}, s32[]{:T(128)}) while((s32[]{:T(128)}, f32[8,64,64]{2,1,0:T(8,128)S(1)}, f32[8,64]{1,0:T(8,128)S(1)}, f32[8,64,64]{2,1,0:T(8,128)S(1)}, s32[]{:T(128)}) %tuple.86), condition=%wide.region_7.8_spmd, body=%wide.region_6.7_spmd.sunk | while | flops 65538 | bytes 919653 | solution.py:107
  50.2 5.4 collective-permute-start
  76.6 5.9 collective-permute-start
  104.6 5.6 collective-permute-start
  114.3 8.7 collective-permute-start
  123.0 8.9 collective-permute-done
  136.3 7.5 collective-permute-done
  143.9 5.6 collective-permute-start
  149.6 7.7 collective-permute-done
  181.8 5.5 collective-permute-start
  190.7 5.3 collective-permute-start
  199.4 5.5 collective-permute-start
  217.2 5.3 collective-permute-start
  227.5 5.5 collective-permute-start
  233.0 5.7 collective-permute-done
  238.9 6.0 collective-permute-start
  275.3 5.3 collective-permute-start
  301.5 5.3 collective-permute-start
  311.6 5.6 collective-permute-start
  317.2 5.7 collective-permute-done
  323.1 6.0 collective-permute-start
  350.4 98.3 %reduce-scatter.2.cloned.1.call-done = f32[16,4096]{1,0:T(8,128)} async-done(((f32[128,4096]{1,0:T(8,128)}), f32[16,4096]{1,0:T(8,128)}) %reduce-scatter.2.cloned.1.call-update) | async-done | bytes 262160 | tf_op jit(solution)/shard_map/reduce_scatter | solution.py:121
  454.9 23.9 %all-reduce = s32[1024]{0:T(1024)S(1)} all-reduce(s32[1024]{0:T(1024)S(1)} %dynamic-update-slice), channel_id=1, replica_groups=mesh['blk'=64,'head'=8] {'blk'}, use_global_device_ids=true, to_apply=%add | all-reduce | flops 1024 | bytes 8192
  478.8 124.2 %all-gather.8.cloned.1.call-done = bf16[1024,4096]{1,0:T(8,128)(2,1)} async-done(((bf16[16,4096]{1,0:T(8,128)(2,1)}), bf16[1024,4096]{1,0:T(8,128)(2,1)}) %all-gather.8.cloned.1.call-update) | async-done | bytes 8388624 | tf_op jit(solution)/shard_map/all_gather | solution.py:131
  603.0 8.2 fusion.38
  611.8 61.3 %all-gather.1 = f32[65536]{0:T(1024)S(1)} all-gather(f32[1024]{0:T(1024)S(1)} %get-tuple-element.237), channel_id=3, replica_groups=mesh['blk'=64,'head'=8] {'blk'}, dimensions={0}, use_global_device_ids=true | all-gather | bytes 266240 | tf_op jit(solution)/shard_map/all_gather | solution.py:17
  673.2 63.6 %all-gather.2 = f32[65536]{0:T(1024)S(1)} all-gather(f32[1024]{0:T(1024)S(1)} %get-tuple-element.236), channel_id=4, replica_groups=mesh['blk'=64,'head'=8] {'blk'}, dimensions={0}, use_global_device_ids=true | all-gather | bytes 266240 | tf_op jit(solution)/shard_map/all_gather | solution.py:17
  736.8 63.0 %all-gather = f32[65536]{0:T(1024)S(1)} all-gather(f32[1024]{0:T(1024)S(1)} %get-tuple-element.289), channel_id=2, replica_groups=mesh['blk'=64,'head'=8] {'blk'}, dimensions={0}, use_global_device_ids=true | all-gather | bytes 266240 | tf_op jit(solution)/shard_map/all_gather | solution.py:17
  799.9 5.9 while.43
  808.4 112.5 %psum.14 = f32[16]{0:T(128)S(1)} all-reduce(f32[16]{0:T(128)S(1)} %compare_select_fusion), channel_id=1, replica_groups=mesh['blk'=64,'head'=8] {'blk'}, use_global_device_ids=true, to_apply=%region_20.21 | all-reduce | flops 16 | bytes 128 | tf_op jit(solution)/shard_map/psum | solution.py:154
  920.9 102.6 %psum.15 = f32[16]{0:T(128)} all-reduce(f32[16]{0:T(128)S(1)} %psum.14), channel_id=1, replica_groups=mesh['blk'=64,'head'=8] {'head'}, use_global_device_ids=true, to_apply=%region_21.22 | all-reduce | flops 16 | bytes 128 | tf_op jit(solution)/shard_map/psum | solution.py:154
  (450 shorter events, 225.4 us)
Async XLA Ops:
  7.2 338.0 %all-gather.6.cloned.1.call-start = ((), (), s32[]{:S(2)}) async-start(), calls=%async_computation.1 | async-start | bytes 4259840 | tf_op jit(solution)/shard_map/all_gather | solution.py:118
  7.9 440.7 %reduce-scatter.2.cloned.1.call-start = ((), (), s32[]{:S(2)}) async-start(), calls=%async_computation.2 | async-start | bytes 2359296 | tf_op jit(solution)/shard_map/reduce_scatter | solution.py:121
  42.0 8.0 collective-permute-start
  50.2 9.0 collective-permute-start
  59.4 8.7 collective-permute-start
  68.2 8.3 collective-permute-start
  76.6 9.4 collective-permute-start
  86.2 8.5 collective-permute-start
  94.8 9.6 collective-permute-start
  104.6 9.6 collective-permute-start
  114.3 17.5 %collective-permute-start = (f32[8,64,64]{2,1,0:T(8,128)S(1)}, f32[8,64,64]{2,1,0:T(8,128)S(1)}, u32[]{:S(2)}, u32[]{:S(2)}) collective-permute-start(f32[8,64,64]{2,1,0:T(8,128)S(1)} %multiply_add_fusion.4), channel_id=1, source_target_pairs={{0,8},{8,16},{16,24},{24,32},{32,40},{40,48},{48,56},{56,64},{64,7... | collective-permute-start | bytes 393224 | tf_op jit(solution)/shard_map/while/body/eval_jaxpr/ppermute | solution.py:13
  132.0 11.8 %collective-permute-start = (f32[8,64,64]{2,1,0:T(8,128)S(1)}, f32[8,64,64]{2,1,0:T(8,128)S(1)}, u32[]{:S(2)}, u32[]{:S(2)}) collective-permute-start(f32[8,64,64]{2,1,0:T(8,128)S(1)} %multiply_add_fusion.4), channel_id=1, source_target_pairs={{0,8},{8,16},{16,24},{24,32},{32,40},{40,48},{48,56},{56,64},{64,7... | collective-permute-start | bytes 393224 | tf_op jit(solution)/shard_map/while/body/eval_jaxpr/ppermute | solution.py:13
  143.9 13.4 %collective-permute-start = (f32[8,64,64]{2,1,0:T(8,128)S(1)}, f32[8,64,64]{2,1,0:T(8,128)S(1)}, u32[]{:S(2)}, u32[]{:S(2)}) collective-permute-start(f32[8,64,64]{2,1,0:T(8,128)S(1)} %multiply_add_fusion.4), channel_id=1, source_target_pairs={{0,8},{8,16},{16,24},{24,32},{32,40},{40,48},{48,56},{56,64},{64,7... | collective-permute-start | bytes 393224 | tf_op jit(solution)/shard_map/while/body/eval_jaxpr/ppermute | solution.py:13
  157.4 8.5 collective-permute-start
  173.7 7.9 collective-permute-start
  181.8 8.8 collective-permute-start
  190.7 8.6 collective-permute-start
  199.4 8.8 collective-permute-start
  208.4 8.7 collective-permute-start
  217.2 10.1 collective-permute-start
  227.5 11.3 %collective-permute-start = (f32[8,64,64]{2,1,0:T(8,128)S(1)}, f32[8,64,64]{2,1,0:T(8,128)S(1)}, u32[]{:S(2)}, u32[]{:S(2)}) collective-permute-start(f32[8,64,64]{2,1,0:T(8,128)S(1)} %multiply_add_fusion.4), channel_id=1, source_target_pairs={{0,8},{8,16},{16,24},{24,32},{32,40},{40,48},{48,56},{56,64},{64,7... | collective-permute-start | bytes 393224 | tf_op jit(solution)/shard_map/while/body/eval_jaxpr/ppermute | solution.py:13
  238.9 11.2 %collective-permute-start = (f32[8,64,64]{2,1,0:T(8,128)S(1)}, f32[8,64,64]{2,1,0:T(8,128)S(1)}, u32[]{:S(2)}, u32[]{:S(2)}) collective-permute-start(f32[8,64,64]{2,1,0:T(8,128)S(1)} %multiply_add_fusion.4), channel_id=1, source_target_pairs={{0,8},{8,16},{16,24},{24,32},{32,40},{40,48},{48,56},{56,64},{64,7... | collective-permute-start | bytes 393224 | tf_op jit(solution)/shard_map/while/body/eval_jaxpr/ppermute | solution.py:13
  250.2 8.8 collective-permute-start
  266.7 8.4 collective-permute-start
  275.3 8.6 collective-permute-start
  284.0 8.6 collective-permute-start
  292.8 8.6 collective-permute-start
  301.5 9.9 collective-permute-start
  311.6 11.4 %collective-permute-start = (f32[8,64,64]{2,1,0:T(8,128)S(1)}, f32[8,64,64]{2,1,0:T(8,128)S(1)}, u32[]{:S(2)}, u32[]{:S(2)}) collective-permute-start(f32[8,64,64]{2,1,0:T(8,128)S(1)} %multiply_add_fusion.4), channel_id=1, source_target_pairs={{0,8},{8,16},{16,24},{24,32},{32,40},{40,48},{48,56},{56,64},{64,7... | collective-permute-start | bytes 393224 | tf_op jit(solution)/shard_map/while/body/eval_jaxpr/ppermute | solution.py:13
  323.1 11.3 %collective-permute-start = (f32[8,64,64]{2,1,0:T(8,128)S(1)}, f32[8,64,64]{2,1,0:T(8,128)S(1)}, u32[]{:S(2)}, u32[]{:S(2)}) collective-permute-start(f32[8,64,64]{2,1,0:T(8,128)S(1)} %multiply_add_fusion.4), channel_id=1, source_target_pairs={{0,8},{8,16},{16,24},{24,32},{32,40},{40,48},{48,56},{56,64},{64,7... | collective-permute-start | bytes 393224 | tf_op jit(solution)/shard_map/while/body/eval_jaxpr/ppermute | solution.py:13
  334.6 8.6 collective-permute-start
  350.3 252.6 %all-gather.8.cloned.1.call-start = ((), (), s32[]{:S(2)}) async-start(), calls=%async_computation.3 | async-start | bytes 8519680 | tf_op jit(solution)/shard_map/all_gather | solution.py:131
  (21 other events, 804.1 us)
Sparse Core Ops, SparseCore 0:
  11.0 147.0 all-gather.5
  350.5 98.1 reduce-scatter.1
  452.8 150.1 all-gather.7
